TPU v7x, 32 devices: a whole 2x2x4 slice. The times are simulated.
32 devices in a mesh: node: 8 (over z, x), feat: 4 (over y, core).
Axes of the slice: x: 2, y: 2, z: 4, core: 2. Of those that a mesh axis runs over, the one named last changes fastest.
Arguments:
- features: bfloat16 [256, 4096], P('feat', 'node'), may hold values from -6 to 6
- tile_values: bfloat16 [256, 128, 128], P('node'), may hold values from -0.1875 to 0.1875
- tile_rows: int32 [64, 4], P('node'), may hold values from 0 to 3
- tile_cols: int32 [64, 4], P('node'), may hold values from 0 to 3
- tile_counts: int32 [64], P('node'), may hold values from 0 to 4, as said below
- weight: bfloat16 [256, 256], replicated, may hold values from -0.375 to 0.375
- cotangent: bfloat16 [256, 4096], P(None, ('node', 'feat')), may hold values from -6 to 6
Outputs:
- activated: bfloat16 [256, 4096], P(None, ('node', 'feat'))
- grad_weight: float32 [256, 256], replicated
- grad_features: float32 [256, 4096], P('feat', 'node')
Inputs may be any that keep to these rules, and one draw needn't show every extreme that they name: `tile_counts`: slots at or past a pair's count are ignored; some pair has all 4 slots live, and the live slots of one receiving node index vary strongly between indices.
All inputs are finite; a program needn't handle non-finite values.
Results may differ from a plain program's by a relative error of at most 0.012.
Values may be sent and summed in bfloat16 or wider, within the bound.
No kernel may reach another device: no remote copies, remote signals or barrier semaphores. Data moves between devices by JAX's collectives and lax.ppermute only.
A program may use at most 64 MiB of HBM per device.

v0:
```python
import jax
import jax.numpy as jnp
from jax import lax
from jax.sharding import PartitionSpec as P


def passed_along(x, axis, by):
    count = lax.axis_size(axis)
    return lax.ppermute(x, axis, [(i, (i + by) % count) for i in range(count)])


def select_pair(tile_values, tile_rows, tile_cols, tile_counts, source):
    slots = tile_rows.shape[1]
    values = lax.dynamic_slice_in_dim(tile_values, source * slots, slots, 0)
    row_ids = lax.dynamic_index_in_dim(tile_rows, source, 0, keepdims=False)
    col_ids = lax.dynamic_index_in_dim(tile_cols, source, 0, keepdims=False)
    number = lax.dynamic_index_in_dim(tile_counts, source, 0, keepdims=False)
    live = (jnp.arange(slots) < number).astype(jnp.float32)
    return (values, row_ids, col_ids, live)


def add_forward(totals, piece, parts, keep):
    values, row_ids, col_ids, live = parts
    blocks_in = piece.reshape(piece.shape[0], -1, values.shape[1])
    block_count = blocks_in.shape[1]
    pick = jax.nn.one_hot(col_ids, block_count, dtype=jnp.bfloat16)
    chosen = jnp.einsum("frm,sr->fsm", blocks_in, pick, preferred_element_type=jnp.float32).astype(
        jnp.bfloat16
    )
    product = jnp.einsum("fsm,sjm->fsj", chosen, values, preferred_element_type=jnp.float32)
    place = jax.nn.one_hot(row_ids, block_count, dtype=jnp.float32) * (live * keep)[:, None]
    return totals + jnp.einsum("fsj,sr->frj", product, place)


def add_backward(totals, grad_blocks, parts, keep):
    values, row_ids, col_ids, live = parts
    block_count = grad_blocks.shape[1]
    pick = jax.nn.one_hot(row_ids, block_count, dtype=jnp.bfloat16)
    chosen = jnp.einsum(
        "frj,sr->fsj", grad_blocks, pick, preferred_element_type=jnp.float32
    ).astype(jnp.bfloat16)
    product = jnp.einsum("fsj,sjm->fsm", chosen, values, preferred_element_type=jnp.float32)
    place = jax.nn.one_hot(col_ids, block_count, dtype=jnp.float32) * (live * keep)[:, None]
    return totals + jnp.einsum("fsm,sc->fcm", product, place)


def per_device(features, tile_values, tile_rows, tile_cols, tile_counts, weight, cotangent):
    node_count = lax.axis_size("node")
    own_index = lax.axis_index("node")
    slice_width = features.shape[0]
    local_nodes = features.shape[1]
    tile_side = tile_values.shape[1]
    block_count = local_nodes // tile_side

    def pair_of(source):
        return select_pair(tile_values, tile_rows, tile_cols, tile_counts, source)

    totals = jnp.zeros((slice_width, block_count, tile_side), jnp.float32)
    totals = add_forward(totals, features, pair_of(own_index), 1.0)

    def ahead_step(step, carry):
        running, moving = carry
        moving = passed_along(moving, "node", 1)
        source = (own_index - step) % node_count
        return (add_forward(running, moving, pair_of(source), 1.0), moving)

    totals, _ = lax.fori_loop(1, node_count, ahead_step, (totals, features))
    aggregated = totals.reshape(slice_width, local_nodes).astype(jnp.bfloat16)
    full_rows = lax.all_to_all(aggregated, "feat", split_axis=1, concat_axis=0, tiled=True)
    pre = jnp.dot(weight.T, full_rows, preferred_element_type=jnp.float32)
    activated = jax.nn.silu(pre).astype(jnp.bfloat16)
    sigma = jax.nn.sigmoid(pre)
    dpre = (cotangent.astype(jnp.float32) * sigma * (1.0 + pre * (1.0 - sigma))).astype(
        jnp.bfloat16
    )
    weight_part = lax.dot_general(
        full_rows, dpre, (((1,), (1,)), ((), ())), preferred_element_type=jnp.float32
    )
    grad_weight = lax.psum(weight_part, ("node", "feat"))
    dagg = jnp.dot(weight, dpre, preferred_element_type=jnp.float32).astype(jnp.bfloat16)
    grad_slices = lax.all_to_all(dagg, "feat", split_axis=0, concat_axis=1, tiled=True)
    grad_blocks = grad_slices.reshape(slice_width, block_count, tile_side)
    zeros = jnp.zeros((slice_width, block_count, tile_side), jnp.float32)
    start = add_backward(zeros, grad_blocks, pair_of((own_index - 1) % node_count), 1.0)

    def carry_step(step, running):
        running = passed_along(running, "node", 1)
        owner = (own_index - step - 1) % node_count
        return add_backward(running, grad_blocks, pair_of(owner), 1.0)

    gradient = lax.fori_loop(1, node_count, carry_step, start)
    return (activated, grad_weight, gradient.reshape(slice_width, local_nodes))


def solution(mesh):
    placed = (
        P("feat", "node"),
        P("node", None, None),
        P("node", None),
        P("node", None),
        P("node"),
        P(),
        P(None, ("node", "feat")),
    )
    return jax.shard_map(
        per_device,
        mesh=mesh,
        in_specs=placed,
        out_specs=(P(None, ("node", "feat")), P(), P("feat", "node")),
        check_vma=False,
    )
```

profile of v0, /device:TPU:0, one launch (start us, length us, event | category | flops | bytes accessed | tf_op | source)
XLA Modules:
  0.0 227.0 jit_solution(9543807741233657913)
XLA Ops:
  7.2 0.9 copy.98
  8.1 0.7 copy-done.2
  11.7 1.1 fusion.47
  12.9 62.7 %while.32 = (s32[]{:T(128)}, f32[64,4,128]{2,1,0:T(4,128)S(1)}, bf16[64,512]{1,0:T(8,128)(2,1)S(1)}, s32[]{:T(128)}, s32[8,4]{1,0:T(8,128)S(1)}, /*index=5*/s32[...) while((s32[]{:T(128)}, f32[64,4,128]{2,1,0:T(4,128)S(1)}, ...), condition=%wide.region_1.2_spmd, body=%wide.region_0.1_spmd.sunk | while | flops 8945741 | bytes 1245694 | solution.py:67
  12.9 3.0 %collective-permute-start = (bf16[64,512]{1,0:T(8,128)(2,1)S(1)}, bf16[64,512]{1,0:T(8,128)(2,1)S(1)}, u32[]{:S(2)}, u32[]{:S(2)}) collective-permute-start(bf16[64,512]{1,0:T(8,128)(2,1)S(1)} %get-tuple-element.610), channel_id=1, source_target_pairs={{0,4},{4,8},{8,12},{12,16},{16,20},{20,24},{24,28},{28,0},{1,5},{5... | collective-permute-start | bytes 196616 | tf_op jit(solution)/shard_map/while/body/eval_jaxpr/ppermute | solution.py:9
  17.2 4.0 %collective-permute-done = bf16[64,512]{1,0:T(8,128)(2,1)S(1)} collective-permute-done((bf16[64,512]{1,0:T(8,128)(2,1)S(1)}, bf16[64,512]{1,0:T(8,128)(2,1)S(1)}, u32[]{:S(2)}, u32[]{:S(2)}) %collective-permute-start) | collective-permute-done | bytes 65568 | tf_op jit(solution)/shard_map/while/body/eval_jaxpr/ppermute | solution.py:9
  21.5 1.1 fusion.115
  24.3 5.7 %collective-permute-done = bf16[64,512]{1,0:T(8,128)(2,1)S(1)} collective-permute-done((bf16[64,512]{1,0:T(8,128)(2,1)S(1)}, bf16[64,512]{1,0:T(8,128)(2,1)S(1)}, u32[]{:S(2)}, u32[]{:S(2)}) %collective-permute-start) | collective-permute-done | bytes 65568 | tf_op jit(solution)/shard_map/while/body/eval_jaxpr/ppermute | solution.py:9
  30.3 1.1 fusion.115
  33.1 5.7 %collective-permute-done = bf16[64,512]{1,0:T(8,128)(2,1)S(1)} collective-permute-done((bf16[64,512]{1,0:T(8,128)(2,1)S(1)}, bf16[64,512]{1,0:T(8,128)(2,1)S(1)}, u32[]{:S(2)}, u32[]{:S(2)}) %collective-permute-start) | collective-permute-done | bytes 65568 | tf_op jit(solution)/shard_map/while/body/eval_jaxpr/ppermute | solution.py:9
  39.0 1.1 fusion.115
  41.9 5.7 %collective-permute-done = bf16[64,512]{1,0:T(8,128)(2,1)S(1)} collective-permute-done((bf16[64,512]{1,0:T(8,128)(2,1)S(1)}, bf16[64,512]{1,0:T(8,128)(2,1)S(1)}, u32[]{:S(2)}, u32[]{:S(2)}) %collective-permute-start) | collective-permute-done | bytes 65568 | tf_op jit(solution)/shard_map/while/body/eval_jaxpr/ppermute | solution.py:9
  47.8 1.1 fusion.115
  50.6 5.7 %collective-permute-done = bf16[64,512]{1,0:T(8,128)(2,1)S(1)} collective-permute-done((bf16[64,512]{1,0:T(8,128)(2,1)S(1)}, bf16[64,512]{1,0:T(8,128)(2,1)S(1)}, u32[]{:S(2)}, u32[]{:S(2)}) %collective-permute-start) | collective-permute-done | bytes 65568 | tf_op jit(solution)/shard_map/while/body/eval_jaxpr/ppermute | solution.py:9
  56.6 1.1 fusion.115
  59.4 5.7 %collective-permute-done = bf16[64,512]{1,0:T(8,128)(2,1)S(1)} collective-permute-done((bf16[64,512]{1,0:T(8,128)(2,1)S(1)}, bf16[64,512]{1,0:T(8,128)(2,1)S(1)}, u32[]{:S(2)}, u32[]{:S(2)}) %collective-permute-start) | collective-permute-done | bytes 65568 | tf_op jit(solution)/shard_map/while/body/eval_jaxpr/ppermute | solution.py:9
  65.3 1.1 fusion.115
  68.2 5.7 %collective-permute-done = bf16[64,512]{1,0:T(8,128)(2,1)S(1)} collective-permute-done((bf16[64,512]{1,0:T(8,128)(2,1)S(1)}, bf16[64,512]{1,0:T(8,128)(2,1)S(1)}, u32[]{:S(2)}, u32[]{:S(2)}) %collective-permute-start) | collective-permute-done | bytes 65568 | tf_op jit(solution)/shard_map/while/body/eval_jaxpr/ppermute | solution.py:9
  74.1 1.1 fusion.115
  76.2 3.4 %all-to-all-start = ((bf16[64,4,128]{2,0,1:T(8,128)(2,1)}), bf16[64,4,128]{2,0,1:T(8,128)(2,1)S(1)}, u32[]{:S(2)}, u32[]{:S(2)}) async-start(bf16[64,4,128]{2,0,1:T(8,128)(2,1)} %copy.71), calls=%async_computation | async-start | bytes 131072 | tf_op jit(solution)/shard_map/all_to_all | solution.py:69
  79.7 0.7 compare_convert_fusion.2
  80.5 3.3 %all-to-all-done = bf16[64,4,128]{2,0,1:T(8,128)(2,1)S(1)} async-done(((bf16[64,4,128]{2,0,1:T(8,128)(2,1)}), bf16[64,4,128]{2,0,1:T(8,128)(2,1)S(1)}, u32[]{:S(2)}, u32[]{:S(2)}) %all-to-all-start) | async-done | bytes 65568 | tf_op jit(solution)/shard_map/all_to_all | solution.py:69
  84.2 0.7 copy.21
  84.9 3.3 %all-to-all-start.1 = ((bf16[4,64,128]{2,1,0:T(8,128)(2,1)}), bf16[4,64,128]{2,1,0:T(8,128)(2,1)S(1)}, u32[]{:S(2)}, u32[]{:S(2)}) async-start(bf16[4,64,128]{2,1,0:T(8,128)(2,1)} %bitcast.30), calls=%async_computation.1 | async-start | bytes 131072 | tf_op jit(solution)/shard_map/all_to_all | solution.py:81
  88.3 0.9 fusion.77
  89.2 0.7 copy.25
  89.9 2.4 %all-to-all-done.1 = bf16[4,64,128]{2,1,0:T(8,128)(2,1)S(1)} async-done(((bf16[4,64,128]{2,1,0:T(8,128)(2,1)}), bf16[4,64,128]{2,1,0:T(8,128)(2,1)S(1)}, u32[]{:S(2)}, u32[]{:S(2)}) %all-to-all-start.1) | async-done | bytes 65568 | tf_op jit(solution)/shard_map/all_to_all | solution.py:81
  92.6 1.1 fusion.45
  93.9 58.6 %while.33 = (s32[]{:T(128)}, f32[64,4,128]{2,1,0:T(4,128)S(1)}, s32[]{:T(128)}, s32[8,4]{1,0:T(8,128)S(1)}, s32[8]{0:T(128)S(1)}, /*index=5*/bf16[32,128,128]{2,...) while((s32[]{:T(128)}, f32[64,4,128]{2,1,0:T(4,128)S(1)}, ...), condition=%wide.region_4.5_spmd, body=%wide.region_3.4_spmd.sunk | while | flops 8945742 | bytes 1245714 | solution.py:91
  94.2 1.1 fusion.125
  96.5 5.2 %collective-permute-done.1 = f32[64,4,128]{2,1,0:T(4,128)S(1)} collective-permute-done((f32[64,4,128]{2,1,0:T(4,128)S(1)}, f32[64,4,128]{2,1,0:T(4,128)S(1)}, u32[]{:S(2)}, u32[]{:S(2)}) %collective-permute-start.1) | collective-permute-done | bytes 131104 | tf_op jit(solution)/shard_map/while/body/eval_jaxpr/ppermute | solution.py:9
  102.5 1.1 fusion.125
  104.8 5.2 %collective-permute-done.1 = f32[64,4,128]{2,1,0:T(4,128)S(1)} collective-permute-done((f32[64,4,128]{2,1,0:T(4,128)S(1)}, f32[64,4,128]{2,1,0:T(4,128)S(1)}, u32[]{:S(2)}, u32[]{:S(2)}) %collective-permute-start.1) | collective-permute-done | bytes 131104 | tf_op jit(solution)/shard_map/while/body/eval_jaxpr/ppermute | solution.py:9
  110.7 1.1 fusion.125
  112.4 0.6 compare_convert_fusion.7
  113.0 5.2 %collective-permute-done.1 = f32[64,4,128]{2,1,0:T(4,128)S(1)} collective-permute-done((f32[64,4,128]{2,1,0:T(4,128)S(1)}, f32[64,4,128]{2,1,0:T(4,128)S(1)}, u32[]{:S(2)}, u32[]{:S(2)}) %collective-permute-start.1) | collective-permute-done | bytes 131104 | tf_op jit(solution)/shard_map/while/body/eval_jaxpr/ppermute | solution.py:9
  118.9 1.1 fusion.125
  120.6 0.6 compare_convert_fusion.7
  121.2 5.1 %collective-permute-done.1 = f32[64,4,128]{2,1,0:T(4,128)S(1)} collective-permute-done((f32[64,4,128]{2,1,0:T(4,128)S(1)}, f32[64,4,128]{2,1,0:T(4,128)S(1)}, u32[]{:S(2)}, u32[]{:S(2)}) %collective-permute-start.1) | collective-permute-done | bytes 131104 | tf_op jit(solution)/shard_map/while/body/eval_jaxpr/ppermute | solution.py:9
  127.0 1.1 fusion.125
  129.3 5.3 %collective-permute-done.1 = f32[64,4,128]{2,1,0:T(4,128)S(1)} collective-permute-done((f32[64,4,128]{2,1,0:T(4,128)S(1)}, f32[64,4,128]{2,1,0:T(4,128)S(1)}, u32[]{:S(2)}, u32[]{:S(2)}) %collective-permute-start.1) | collective-permute-done | bytes 131104 | tf_op jit(solution)/shard_map/while/body/eval_jaxpr/ppermute | solution.py:9
  135.4 1.1 fusion.125
  137.7 6.3 %collective-permute-done.1 = f32[64,4,128]{2,1,0:T(4,128)S(1)} collective-permute-done((f32[64,4,128]{2,1,0:T(4,128)S(1)}, f32[64,4,128]{2,1,0:T(4,128)S(1)}, u32[]{:S(2)}, u32[]{:S(2)}) %collective-permute-start.1) | collective-permute-done | bytes 131104 | tf_op jit(solution)/shard_map/while/body/eval_jaxpr/ppermute | solution.py:9
  144.7 1.1 fusion.125
  147.0 5.2 %collective-permute-done.1 = f32[64,4,128]{2,1,0:T(4,128)S(1)} collective-permute-done((f32[64,4,128]{2,1,0:T(4,128)S(1)}, f32[64,4,128]{2,1,0:T(4,128)S(1)}, u32[]{:S(2)}, u32[]{:S(2)}) %collective-permute-start.1) | collective-permute-done | bytes 131104 | tf_op jit(solution)/shard_map/while/body/eval_jaxpr/ppermute | solution.py:9
  152.5 0.7 copy.72
  153.2 65.3 %all-reduce.2.cloned.1.call-done = f32[256,256]{1,0:T(8,128)} async-done(((f32[256,256]{1,0:T(8,128)}), f32[256,256]{1,0:T(8,128)}) %all-reduce.2.cloned.1.call-update) | async-done | bytes 262160 | tf_op jit(solution)/shard_map/psum | solution.py:79
  218.5 1.7 copy.99
  (121 shorter events, 30.4 us)
Async XLA Ops:
  7.2 76.6 %copy-start = (bf16[256,256]{1,0:T(8,128)(2,1)S(1)}, bf16[256,256]{1,0:T(8,128)(2,1)}, u32[]{:S(2)}) copy-start(bf16[256,256]{1,0:T(8,128)(2,1)} %param.16) | copy-start | bytes 393220
  8.1 0.7 copy-start.2
  8.7 0.7 copy-start.3
  9.5 0.7 copy-start.4
  12.9 8.3 %collective-permute-start = (bf16[64,512]{1,0:T(8,128)(2,1)S(1)}, bf16[64,512]{1,0:T(8,128)(2,1)S(1)}, u32[]{:S(2)}, u32[]{:S(2)}) collective-permute-start(bf16[64,512]{1,0:T(8,128)(2,1)S(1)} %get-tuple-element.610), channel_id=1, source_target_pairs={{0,4},{4,8},{8,12},{12,16},{16,20},{20,24},{24,28},{28,0},{1,5},{5... | collective-permute-start | bytes 196616 | tf_op jit(solution)/shard_map/while/body/eval_jaxpr/ppermute | solution.py:9
  23.0 7.0 %collective-permute-start = (bf16[64,512]{1,0:T(8,128)(2,1)S(1)}, bf16[64,512]{1,0:T(8,128)(2,1)S(1)}, u32[]{:S(2)}, u32[]{:S(2)}) collective-permute-start(bf16[64,512]{1,0:T(8,128)(2,1)S(1)} %get-tuple-element.610), channel_id=1, source_target_pairs={{0,4},{4,8},{8,12},{12,16},{16,20},{20,24},{24,28},{28,0},{1,5},{5... | collective-permute-start | bytes 196616 | tf_op jit(solution)/shard_map/while/body/eval_jaxpr/ppermute | solution.py:9
  31.7 7.0 %collective-permute-start = (bf16[64,512]{1,0:T(8,128)(2,1)S(1)}, bf16[64,512]{1,0:T(8,128)(2,1)S(1)}, u32[]{:S(2)}, u32[]{:S(2)}) collective-permute-start(bf16[64,512]{1,0:T(8,128)(2,1)S(1)} %get-tuple-element.610), channel_id=1, source_target_pairs={{0,4},{4,8},{8,12},{12,16},{16,20},{20,24},{24,28},{28,0},{1,5},{5... | collective-permute-start | bytes 196616 | tf_op jit(solution)/shard_map/while/body/eval_jaxpr/ppermute | solution.py:9
  40.5 7.0 %collective-permute-start = (bf16[64,512]{1,0:T(8,128)(2,1)S(1)}, bf16[64,512]{1,0:T(8,128)(2,1)S(1)}, u32[]{:S(2)}, u32[]{:S(2)}) collective-permute-start(bf16[64,512]{1,0:T(8,128)(2,1)S(1)} %get-tuple-element.610), channel_id=1, source_target_pairs={{0,4},{4,8},{8,12},{12,16},{16,20},{20,24},{24,28},{28,0},{1,5},{5... | collective-permute-start | bytes 196616 | tf_op jit(solution)/shard_map/while/body/eval_jaxpr/ppermute | solution.py:9
  49.3 7.0 %collective-permute-start = (bf16[64,512]{1,0:T(8,128)(2,1)S(1)}, bf16[64,512]{1,0:T(8,128)(2,1)S(1)}, u32[]{:S(2)}, u32[]{:S(2)}) collective-permute-start(bf16[64,512]{1,0:T(8,128)(2,1)S(1)} %get-tuple-element.610), channel_id=1, source_target_pairs={{0,4},{4,8},{8,12},{12,16},{16,20},{20,24},{24,28},{28,0},{1,5},{5... | collective-permute-start | bytes 196616 | tf_op jit(solution)/shard_map/while/body/eval_jaxpr/ppermute | solution.py:9
  58.1 7.0 %collective-permute-start = (bf16[64,512]{1,0:T(8,128)(2,1)S(1)}, bf16[64,512]{1,0:T(8,128)(2,1)S(1)}, u32[]{:S(2)}, u32[]{:S(2)}) collective-permute-start(bf16[64,512]{1,0:T(8,128)(2,1)S(1)} %get-tuple-element.610), channel_id=1, source_target_pairs={{0,4},{4,8},{8,12},{12,16},{16,20},{20,24},{24,28},{28,0},{1,5},{5... | collective-permute-start | bytes 196616 | tf_op jit(solution)/shard_map/while/body/eval_jaxpr/ppermute | solution.py:9
  66.8 7.0 %collective-permute-start = (bf16[64,512]{1,0:T(8,128)(2,1)S(1)}, bf16[64,512]{1,0:T(8,128)(2,1)S(1)}, u32[]{:S(2)}, u32[]{:S(2)}) collective-permute-start(bf16[64,512]{1,0:T(8,128)(2,1)S(1)} %get-tuple-element.610), channel_id=1, source_target_pairs={{0,4},{4,8},{8,12},{12,16},{16,20},{20,24},{24,28},{28,0},{1,5},{5... | collective-permute-start | bytes 196616 | tf_op jit(solution)/shard_map/while/body/eval_jaxpr/ppermute | solution.py:9
  76.2 4.1 %copy-start.1 = (bf16[256,128]{1,0:T(8,128)(2,1)S(1)}, bf16[256,128]{1,0:T(8,128)(2,1)}, u32[]{:S(2)}) copy-start(bf16[256,128]{1,0:T(8,128)(2,1)} %param.17) | copy-start | bytes 196612
  76.2 7.5 %all-to-all-start = ((bf16[64,4,128]{2,0,1:T(8,128)(2,1)}), bf16[64,4,128]{2,0,1:T(8,128)(2,1)S(1)}, u32[]{:S(2)}, u32[]{:S(2)}) async-start(bf16[64,4,128]{2,0,1:T(8,128)(2,1)} %copy.71), calls=%async_computation | async-start | bytes 131072 | tf_op jit(solution)/shard_map/all_to_all | solution.py:69
  84.9 7.4 %all-to-all-start.1 = ((bf16[4,64,128]{2,1,0:T(8,128)(2,1)}), bf16[4,64,128]{2,1,0:T(8,128)(2,1)S(1)}, u32[]{:S(2)}, u32[]{:S(2)}) async-start(bf16[4,64,128]{2,1,0:T(8,128)(2,1)} %bitcast.30), calls=%async_computation.1 | async-start | bytes 131072 | tf_op jit(solution)/shard_map/all_to_all | solution.py:81
  88.2 130.3 %all-reduce.2.cloned.1.call-start = ((), (), s32[]{:S(2)}) async-start(), calls=%async_computation.2 | async-start | bytes 524288 | tf_op jit(solution)/shard_map/psum | solution.py:79
  93.9 7.9 %collective-permute-start.1 = (f32[64,4,128]{2,1,0:T(4,128)S(1)}, f32[64,4,128]{2,1,0:T(4,128)S(1)}, u32[]{:S(2)}, u32[]{:S(2)}) collective-permute-start(f32[64,4,128]{2,1,0:T(4,128)S(1)} %get-tuple-element.652), channel_id=1, source_target_pairs={{0,4},{4,8},{8,12},{12,16},{16,20},{20,24},{24,28},{28,0},{1,5},{5... | collective-permute-start | bytes 393224 | tf_op jit(solution)/shard_map/while/body/eval_jaxpr/ppermute | solution.py:9
  102.1 7.9 %collective-permute-start.1 = (f32[64,4,128]{2,1,0:T(4,128)S(1)}, f32[64,4,128]{2,1,0:T(4,128)S(1)}, u32[]{:S(2)}, u32[]{:S(2)}) collective-permute-start(f32[64,4,128]{2,1,0:T(4,128)S(1)} %get-tuple-element.652), channel_id=1, source_target_pairs={{0,4},{4,8},{8,12},{12,16},{16,20},{20,24},{24,28},{28,0},{1,5},{5... | collective-permute-start | bytes 393224 | tf_op jit(solution)/shard_map/while/body/eval_jaxpr/ppermute | solution.py:9
  110.4 7.9 %collective-permute-start.1 = (f32[64,4,128]{2,1,0:T(4,128)S(1)}, f32[64,4,128]{2,1,0:T(4,128)S(1)}, u32[]{:S(2)}, u32[]{:S(2)}) collective-permute-start(f32[64,4,128]{2,1,0:T(4,128)S(1)} %get-tuple-element.652), channel_id=1, source_target_pairs={{0,4},{4,8},{8,12},{12,16},{16,20},{20,24},{24,28},{28,0},{1,5},{5... | collective-permute-start | bytes 393224 | tf_op jit(solution)/shard_map/while/body/eval_jaxpr/ppermute | solution.py:9
  118.6 7.7 %collective-permute-start.1 = (f32[64,4,128]{2,1,0:T(4,128)S(1)}, f32[64,4,128]{2,1,0:T(4,128)S(1)}, u32[]{:S(2)}, u32[]{:S(2)}) collective-permute-start(f32[64,4,128]{2,1,0:T(4,128)S(1)} %get-tuple-element.652), channel_id=1, source_target_pairs={{0,4},{4,8},{8,12},{12,16},{16,20},{20,24},{24,28},{28,0},{1,5},{5... | collective-permute-start | bytes 393224 | tf_op jit(solution)/shard_map/while/body/eval_jaxpr/ppermute | solution.py:9
  126.7 8.0 %collective-permute-start.1 = (f32[64,4,128]{2,1,0:T(4,128)S(1)}, f32[64,4,128]{2,1,0:T(4,128)S(1)}, u32[]{:S(2)}, u32[]{:S(2)}) collective-permute-start(f32[64,4,128]{2,1,0:T(4,128)S(1)} %get-tuple-element.652), channel_id=1, source_target_pairs={{0,4},{4,8},{8,12},{12,16},{16,20},{20,24},{24,28},{28,0},{1,5},{5... | collective-permute-start | bytes 393224 | tf_op jit(solution)/shard_map/while/body/eval_jaxpr/ppermute | solution.py:9
  135.0 8.9 %collective-permute-start.1 = (f32[64,4,128]{2,1,0:T(4,128)S(1)}, f32[64,4,128]{2,1,0:T(4,128)S(1)}, u32[]{:S(2)}, u32[]{:S(2)}) collective-permute-start(f32[64,4,128]{2,1,0:T(4,128)S(1)} %get-tuple-element.652), channel_id=1, source_target_pairs={{0,4},{4,8},{8,12},{12,16},{16,20},{20,24},{24,28},{28,0},{1,5},{5... | collective-permute-start | bytes 393224 | tf_op jit(solution)/shard_map/while/body/eval_jaxpr/ppermute | solution.py:9
  144.3 7.8 %collective-permute-start.1 = (f32[64,4,128]{2,1,0:T(4,128)S(1)}, f32[64,4,128]{2,1,0:T(4,128)S(1)}, u32[]{:S(2)}, u32[]{:S(2)}) collective-permute-start(f32[64,4,128]{2,1,0:T(4,128)S(1)} %get-tuple-element.652), channel_id=1, source_target_pairs={{0,4},{4,8},{8,12},{12,16},{16,20},{20,24},{24,28},{28,0},{1,5},{5... | collective-permute-start | bytes 393224 | tf_op jit(solution)/shard_map/while/body/eval_jaxpr/ppermute | solution.py:9
Sparse Core Ops, SparseCore 0:
  95.1 123.3 all-reduce.1
where the time goes:
time: 228 us; the launch traced here: 227 us
  waiting for transfers between devices  147 us (64%)
  matrix products  27.7 us (12%)
  local copies, waits for them, and re-layouts  16.8 us (7%)
  between operations  14.2 us (6%)
  starting transfers between devices  10.5 us (5%)
  other arithmetic  10.4 us (5%)
    ppermute x14, waiting for transfers between devices, passed_along(): return lax.ppermute(x, axis, [(i, (i + by) % count) for i in range(count)])  75.5 us
    psum x1, waiting for transfers between devices, per_device(): grad_weight = lax.psum(weight_part, ('node', 'feat'))  65.3 us
    convert_element_type x16, other arithmetic, select_pair(): live = (jnp.arange(slots) < number).astype(jnp.float32)  10.4 us
    dynamic_slice x15, local copies, waits for them, and re-layouts, select_pair(): number = lax.dynamic_index_in_dim(tile_counts, source, 0, keepdims=False)  8.87 us
    dot_general x8, matrix products, add_forward(): jnp.einsum('fsm,sjm->fsj', chosen, values, preferred_element_type=jnp.flo...  8.64 us
    dot_general x8, matrix products, add_backward(): jnp.einsum('fsj,sjm->fsm', chosen, values, preferred_element_type=jnp.flo...  8.47 us
    unnamed x15, local copies, waits for them, and re-layouts  5.78 us
  transfers between devices with their start and end apart: 17, of which 17 were waited for; matrix products, arithmetic and copies ran while one was open for 15% of the time, Pallas kernels for 0%

commit v1 on v0

--- a/solution.py
+++ b/solution.py
@@ -76,7 +76,7 @@
     weight_part = lax.dot_general(
         full_rows, dpre, (((1,), (1,)), ((), ())), preferred_element_type=jnp.float32
     )
-    grad_weight = lax.psum(weight_part, ("node", "feat"))
+    grad_weight = jnp.sum(lax.all_gather(weight_part, ("node", "feat")), axis=0)
     dagg = jnp.dot(weight, dpre, preferred_element_type=jnp.float32).astype(jnp.bfloat16)
     grad_slices = lax.all_to_all(dagg, "feat", split_axis=0, concat_axis=1, tiled=True)
     grad_blocks = grad_slices.reshape(slice_width, block_count, tile_side)

time: 228 us -> 184 us (0.81)
  waiting for transfers between devices: 147 us -> 87.3 us
  local copies, waits for them, and re-layouts: 16.8 us -> 26.2 us
  other arithmetic: 10.4 us -> 14.9 us
    psum x1 -> x0, waiting for transfers between devices: 65.3 us -> none  [per_device(): grad_weight = lax.psum(weight_part, ('node', 'feat'))]
    dynamic_slice x15, local copies, waits for them, and re-layouts: 8.87 us -> 18.8 us  [select_pair(): number = lax.dynamic_index_in_dim(tile_counts, source, 0, keepdims=False)]
    reduce_sum x0 -> x1, other arithmetic: none -> 4.63 us  [per_device(): grad_weight = jnp.sum(lax.all_gather(weight_part, ('node', 'feat')), axis=0)]
    ppermute x14, waiting for transfers between devices: 75.5 us -> 79.9 us  [passed_along(): return lax.ppermute(x, axis, [(i, (i + by) % count) for i in range(count)])]
    unnamed x15 -> x6, local copies, waits for them, and re-layouts: 5.78 us -> 3.23 us
  transfers between devices with their start and end apart: 17 -> 17, of which waited for: 17 -> 17; matrix products, arithmetic and copies ran while one was open for 15% -> 24% of each run, Pallas kernels for 0% -> 0%
where the time goes in v1:
time: 184 us; the launch traced here: 182 us
  waiting for transfers between devices  87.3 us (47%)
  matrix products  27.7 us (15%)
  local copies, waits for them, and re-layouts  26.2 us (14%)
  other arithmetic  14.9 us (8%)
  between operations  14.2 us (8%)
  starting transfers between devices  10.4 us (6%)
    ppermute x14, waiting for transfers between devices, passed_along(): return lax.ppermute(x, axis, [(i, (i + by) % count) for i in range(count)])  79.9 us
    dynamic_slice x15, local copies, waits for them, and re-layouts, select_pair(): number = lax.dynamic_index_in_dim(tile_counts, source, 0, keepdims=False)  18.8 us
    convert_element_type x16, other arithmetic, select_pair(): live = (jnp.arange(slots) < number).astype(jnp.float32)  10.3 us
    dot_general x8, matrix products, add_forward(): jnp.einsum('fsm,sjm->fsj', chosen, values, preferred_element_type=jnp.flo...  8.63 us
    dot_general x8, matrix products, add_backward(): jnp.einsum('fsj,sjm->fsm', chosen, values, preferred_element_type=jnp.flo...  8.5 us
    reduce_sum x1, other arithmetic, per_device(): grad_weight = jnp.sum(lax.all_gather(weight_part, ('node', 'feat')), axis=0)  4.63 us
    ppermute x14, starting transfers between devices, passed_along(): return lax.ppermute(x, axis, [(i, (i + by) % count) for i in range(count)])  3.75 us
  transfers between devices with their start and end apart: 17, of which 17 were waited for; matrix products, arithmetic and copies ran while one was open for 24% of the time, Pallas kernels for 0%

profile of v1, /device:TPU:0, one launch (start us, length us, event | category | flops | bytes accessed | tf_op | source)
XLA Modules:
  0.0 181.6 jit_solution(3731943378391240382)
XLA Ops:
  10.6 1.3 fusion.76
  12.8 1.1 fusion.47
  14.1 62.6 %while.32 = (s32[]{:T(128)}, f32[64,4,128]{2,1,0:T(4,128)S(1)}, bf16[64,512]{1,0:T(8,128)(2,1)S(1)}, s32[]{:T(128)}, s32[8,4]{1,0:T(8,128)S(1)}, /*index=5*/s32[...) while((s32[]{:T(128)}, f32[64,4,128]{2,1,0:T(4,128)S(1)}, ...), condition=%wide.region_1.2_spmd, body=%wide.region_0.1_spmd.sunk | while | flops 8945741 | bytes 1245694 | solution.py:67
  14.1 3.0 %collective-permute-start = (bf16[64,512]{1,0:T(8,128)(2,1)S(1)}, bf16[64,512]{1,0:T(8,128)(2,1)S(1)}, u32[]{:S(2)}, u32[]{:S(2)}) collective-permute-start(bf16[64,512]{1,0:T(8,128)(2,1)S(1)} %get-tuple-element.610), channel_id=1, source_target_pairs={{0,4},{4,8},{8,12},{12,16},{16,20},{20,24},{24,28},{28,0},{1,5},{5... | collective-permute-start | bytes 196616 | tf_op jit(solution)/shard_map/while/body/eval_jaxpr/ppermute | solution.py:9
  17.1 1.2 dynamic_slice.148
  19.0 3.4 %collective-permute-done = bf16[64,512]{1,0:T(8,128)(2,1)S(1)} collective-permute-done((bf16[64,512]{1,0:T(8,128)(2,1)S(1)}, bf16[64,512]{1,0:T(8,128)(2,1)S(1)}, u32[]{:S(2)}, u32[]{:S(2)}) %collective-permute-start) | collective-permute-done | bytes 65568 | tf_op jit(solution)/shard_map/while/body/eval_jaxpr/ppermute | solution.py:9
  22.6 1.1 fusion.115
  24.2 1.2 dynamic_slice.148
  26.1 5.0 %collective-permute-done = bf16[64,512]{1,0:T(8,128)(2,1)S(1)} collective-permute-done((bf16[64,512]{1,0:T(8,128)(2,1)S(1)}, bf16[64,512]{1,0:T(8,128)(2,1)S(1)}, u32[]{:S(2)}, u32[]{:S(2)}) %collective-permute-start) | collective-permute-done | bytes 65568 | tf_op jit(solution)/shard_map/while/body/eval_jaxpr/ppermute | solution.py:9
  31.4 1.1 fusion.115
  33.0 1.2 dynamic_slice.148
  34.9 5.0 %collective-permute-done = bf16[64,512]{1,0:T(8,128)(2,1)S(1)} collective-permute-done((bf16[64,512]{1,0:T(8,128)(2,1)S(1)}, bf16[64,512]{1,0:T(8,128)(2,1)S(1)}, u32[]{:S(2)}, u32[]{:S(2)}) %collective-permute-start) | collective-permute-done | bytes 65568 | tf_op jit(solution)/shard_map/while/body/eval_jaxpr/ppermute | solution.py:9
  40.1 1.1 fusion.115
  41.7 1.2 dynamic_slice.148
  43.6 5.0 %collective-permute-done = bf16[64,512]{1,0:T(8,128)(2,1)S(1)} collective-permute-done((bf16[64,512]{1,0:T(8,128)(2,1)S(1)}, bf16[64,512]{1,0:T(8,128)(2,1)S(1)}, u32[]{:S(2)}, u32[]{:S(2)}) %collective-permute-start) | collective-permute-done | bytes 65568 | tf_op jit(solution)/shard_map/while/body/eval_jaxpr/ppermute | solution.py:9
  48.9 1.1 fusion.115
  50.5 1.2 dynamic_slice.148
  52.4 5.0 %collective-permute-done = bf16[64,512]{1,0:T(8,128)(2,1)S(1)} collective-permute-done((bf16[64,512]{1,0:T(8,128)(2,1)S(1)}, bf16[64,512]{1,0:T(8,128)(2,1)S(1)}, u32[]{:S(2)}, u32[]{:S(2)}) %collective-permute-start) | collective-permute-done | bytes 65568 | tf_op jit(solution)/shard_map/while/body/eval_jaxpr/ppermute | solution.py:9
  57.7 1.1 fusion.115
  59.3 1.2 dynamic_slice.148
  61.2 5.0 %collective-permute-done = bf16[64,512]{1,0:T(8,128)(2,1)S(1)} collective-permute-done((bf16[64,512]{1,0:T(8,128)(2,1)S(1)}, bf16[64,512]{1,0:T(8,128)(2,1)S(1)}, u32[]{:S(2)}, u32[]{:S(2)}) %collective-permute-start) | collective-permute-done | bytes 65568 | tf_op jit(solution)/shard_map/while/body/eval_jaxpr/ppermute | solution.py:9
  66.5 1.1 fusion.115
  68.0 1.2 dynamic_slice.148
  70.0 5.0 %collective-permute-done = bf16[64,512]{1,0:T(8,128)(2,1)S(1)} collective-permute-done((bf16[64,512]{1,0:T(8,128)(2,1)S(1)}, bf16[64,512]{1,0:T(8,128)(2,1)S(1)}, u32[]{:S(2)}, u32[]{:S(2)}) %collective-permute-start) | collective-permute-done | bytes 65568 | tf_op jit(solution)/shard_map/while/body/eval_jaxpr/ppermute | solution.py:9
  75.2 1.1 fusion.115
  77.4 3.3 %all-to-all-start = ((bf16[64,4,128]{2,0,1:T(8,128)(2,1)}), bf16[64,4,128]{2,0,1:T(8,128)(2,1)S(1)}, u32[]{:S(2)}, u32[]{:S(2)}) async-start(bf16[64,4,128]{2,0,1:T(8,128)(2,1)} %copy.71), calls=%async_computation | async-start | bytes 131072 | tf_op jit(solution)/shard_map/all_to_all | solution.py:69
  81.7 3.1 %all-to-all-done = bf16[64,4,128]{2,0,1:T(8,128)(2,1)S(1)} async-done(((bf16[64,4,128]{2,0,1:T(8,128)(2,1)}), bf16[64,4,128]{2,0,1:T(8,128)(2,1)S(1)}, u32[]{:S(2)}, u32[]{:S(2)}) %all-to-all-start) | async-done | bytes 65568 | tf_op jit(solution)/shard_map/all_to_all | solution.py:69
  86.8 3.3 %all-to-all-start.1 = ((bf16[4,64,128]{2,1,0:T(8,128)(2,1)}), bf16[4,64,128]{2,1,0:T(8,128)(2,1)S(1)}, u32[]{:S(2)}, u32[]{:S(2)}) async-start(bf16[4,64,128]{2,1,0:T(8,128)(2,1)} %bitcast.31), calls=%async_computation.1 | async-start | bytes 131072 | tf_op jit(solution)/shard_map/all_to_all | solution.py:81
  91.4 3.0 %all-to-all-done.1 = bf16[4,64,128]{2,1,0:T(8,128)(2,1)S(1)} async-done(((bf16[4,64,128]{2,1,0:T(8,128)(2,1)}), bf16[4,64,128]{2,1,0:T(8,128)(2,1)S(1)}, u32[]{:S(2)}, u32[]{:S(2)}) %all-to-all-start.1) | async-done | bytes 65568 | tf_op jit(solution)/shard_map/all_to_all | solution.py:81
  95.9 72.2 %while.33 = (s32[]{:T(128)}, f32[64,4,128]{2,1,0:T(4,128)S(1)}, s32[]{:T(128)}, s32[8,4]{1,0:T(8,128)S(1)}, s32[8]{0:T(128)}, /*index=5*/bf16[32,128,128]{2,1,0:...) while((s32[]{:T(128)}, f32[64,4,128]{2,1,0:T(4,128)S(1)}, ...), condition=%wide.region_4.5_spmd, body=%wide.region_3.4_spmd.sunk | while | flops 8945742 | bytes 1245714 | solution.py:91
  97.4 1.3 dynamic_slice.151
  99.3 7.5 %collective-permute-done.1 = f32[64,4,128]{2,1,0:T(4,128)S(1)} collective-permute-done((f32[64,4,128]{2,1,0:T(4,128)S(1)}, f32[64,4,128]{2,1,0:T(4,128)S(1)}, u32[]{:S(2)}, u32[]{:S(2)}) %collective-permute-start.1) | collective-permute-done | bytes 131104 | tf_op jit(solution)/shard_map/while/body/eval_jaxpr/ppermute | solution.py:9
  108.6 1.3 dynamic_slice.151
  110.5 4.5 %collective-permute-done.1 = f32[64,4,128]{2,1,0:T(4,128)S(1)} collective-permute-done((f32[64,4,128]{2,1,0:T(4,128)S(1)}, f32[64,4,128]{2,1,0:T(4,128)S(1)}, u32[]{:S(2)}, u32[]{:S(2)}) %collective-permute-start.1) | collective-permute-done | bytes 131104 | tf_op jit(solution)/shard_map/while/body/eval_jaxpr/ppermute | solution.py:9
  116.8 1.3 dynamic_slice.151
  118.7 6.2 %collective-permute-done.1 = f32[64,4,128]{2,1,0:T(4,128)S(1)} collective-permute-done((f32[64,4,128]{2,1,0:T(4,128)S(1)}, f32[64,4,128]{2,1,0:T(4,128)S(1)}, u32[]{:S(2)}, u32[]{:S(2)}) %collective-permute-start.1) | collective-permute-done | bytes 131104 | tf_op jit(solution)/shard_map/while/body/eval_jaxpr/ppermute | solution.py:9
  125.6 1.1 fusion.125
  126.7 1.3 dynamic_slice.151
  128.6 6.4 %collective-permute-done.1 = f32[64,4,128]{2,1,0:T(4,128)S(1)} collective-permute-done((f32[64,4,128]{2,1,0:T(4,128)S(1)}, f32[64,4,128]{2,1,0:T(4,128)S(1)}, u32[]{:S(2)}, u32[]{:S(2)}) %collective-permute-start.1) | collective-permute-done | bytes 131104 | tf_op jit(solution)/shard_map/while/body/eval_jaxpr/ppermute | solution.py:9
  136.8 1.3 dynamic_slice.151
  138.7 7.1 %collective-permute-done.1 = f32[64,4,128]{2,1,0:T(4,128)S(1)} collective-permute-done((f32[64,4,128]{2,1,0:T(4,128)S(1)}, f32[64,4,128]{2,1,0:T(4,128)S(1)}, u32[]{:S(2)}, u32[]{:S(2)}) %collective-permute-start.1) | collective-permute-done | bytes 131104 | tf_op jit(solution)/shard_map/while/body/eval_jaxpr/ppermute | solution.py:9
  147.6 1.3 dynamic_slice.151
  149.5 7.6 %collective-permute-done.1 = f32[64,4,128]{2,1,0:T(4,128)S(1)} collective-permute-done((f32[64,4,128]{2,1,0:T(4,128)S(1)}, f32[64,4,128]{2,1,0:T(4,128)S(1)}, u32[]{:S(2)}, u32[]{:S(2)}) %collective-permute-start.1) | collective-permute-done | bytes 131104 | tf_op jit(solution)/shard_map/while/body/eval_jaxpr/ppermute | solution.py:9
  157.8 1.1 fusion.125
  158.9 1.2 dynamic_slice.151
  160.8 7.0 %collective-permute-done.1 = f32[64,4,128]{2,1,0:T(4,128)S(1)} collective-permute-done((f32[64,4,128]{2,1,0:T(4,128)S(1)}, f32[64,4,128]{2,1,0:T(4,128)S(1)}, u32[]{:S(2)}, u32[]{:S(2)}) %collective-permute-start.1) | collective-permute-done | bytes 131104 | tf_op jit(solution)/shard_map/while/body/eval_jaxpr/ppermute | solution.py:9
  168.8 1.3 all-gather.3.cloned.1.call-done
  170.2 4.6 %reduce_sum.9 = f32[256,256]{1,0:T(8,128)} reduce(f32[32,256,256]{2,1,0:T(8,128)} %bitcast.127, f32[]{:T(128)} %constant.199.clone.1), dimensions={0}, to_apply=%region_2.3 | reduce | flops 2031616 | bytes 8650756 | tf_op jit(solution)/shard_map/reduce_sum | solution.py:79
  (113 shorter events, 35.5 us)
Async XLA Ops:
  7.2 77.6 %copy-start = (bf16[256,256]{1,0:T(8,128)(2,1)S(1)}, bf16[256,256]{1,0:T(8,128)(2,1)}, u32[]{:S(2)}) copy-start(bf16[256,256]{1,0:T(8,128)(2,1)} %param.16) | copy-start | bytes 393220
  14.1 8.3 %collective-permute-start = (bf16[64,512]{1,0:T(8,128)(2,1)S(1)}, bf16[64,512]{1,0:T(8,128)(2,1)S(1)}, u32[]{:S(2)}, u32[]{:S(2)}) collective-permute-start(bf16[64,512]{1,0:T(8,128)(2,1)S(1)} %get-tuple-element.610), channel_id=1, source_target_pairs={{0,4},{4,8},{8,12},{12,16},{16,20},{20,24},{24,28},{28,0},{1,5},{5... | collective-permute-start | bytes 196616 | tf_op jit(solution)/shard_map/while/body/eval_jaxpr/ppermute | solution.py:9
  24.1 7.0 %collective-permute-start = (bf16[64,512]{1,0:T(8,128)(2,1)S(1)}, bf16[64,512]{1,0:T(8,128)(2,1)S(1)}, u32[]{:S(2)}, u32[]{:S(2)}) collective-permute-start(bf16[64,512]{1,0:T(8,128)(2,1)S(1)} %get-tuple-element.610), channel_id=1, source_target_pairs={{0,4},{4,8},{8,12},{12,16},{16,20},{20,24},{24,28},{28,0},{1,5},{5... | collective-permute-start | bytes 196616 | tf_op jit(solution)/shard_map/while/body/eval_jaxpr/ppermute | solution.py:9
  32.9 7.0 %collective-permute-start = (bf16[64,512]{1,0:T(8,128)(2,1)S(1)}, bf16[64,512]{1,0:T(8,128)(2,1)S(1)}, u32[]{:S(2)}, u32[]{:S(2)}) collective-permute-start(bf16[64,512]{1,0:T(8,128)(2,1)S(1)} %get-tuple-element.610), channel_id=1, source_target_pairs={{0,4},{4,8},{8,12},{12,16},{16,20},{20,24},{24,28},{28,0},{1,5},{5... | collective-permute-start | bytes 196616 | tf_op jit(solution)/shard_map/while/body/eval_jaxpr/ppermute | solution.py:9
  41.6 7.0 %collective-permute-start = (bf16[64,512]{1,0:T(8,128)(2,1)S(1)}, bf16[64,512]{1,0:T(8,128)(2,1)S(1)}, u32[]{:S(2)}, u32[]{:S(2)}) collective-permute-start(bf16[64,512]{1,0:T(8,128)(2,1)S(1)} %get-tuple-element.610), channel_id=1, source_target_pairs={{0,4},{4,8},{8,12},{12,16},{16,20},{20,24},{24,28},{28,0},{1,5},{5... | collective-permute-start | bytes 196616 | tf_op jit(solution)/shard_map/while/body/eval_jaxpr/ppermute | solution.py:9
  50.4 7.0 %collective-permute-start = (bf16[64,512]{1,0:T(8,128)(2,1)S(1)}, bf16[64,512]{1,0:T(8,128)(2,1)S(1)}, u32[]{:S(2)}, u32[]{:S(2)}) collective-permute-start(bf16[64,512]{1,0:T(8,128)(2,1)S(1)} %get-tuple-element.610), channel_id=1, source_target_pairs={{0,4},{4,8},{8,12},{12,16},{16,20},{20,24},{24,28},{28,0},{1,5},{5... | collective-permute-start | bytes 196616 | tf_op jit(solution)/shard_map/while/body/eval_jaxpr/ppermute | solution.py:9
  59.2 7.0 %collective-permute-start = (bf16[64,512]{1,0:T(8,128)(2,1)S(1)}, bf16[64,512]{1,0:T(8,128)(2,1)S(1)}, u32[]{:S(2)}, u32[]{:S(2)}) collective-permute-start(bf16[64,512]{1,0:T(8,128)(2,1)S(1)} %get-tuple-element.610), channel_id=1, source_target_pairs={{0,4},{4,8},{8,12},{12,16},{16,20},{20,24},{24,28},{28,0},{1,5},{5... | collective-permute-start | bytes 196616 | tf_op jit(solution)/shard_map/while/body/eval_jaxpr/ppermute | solution.py:9
  68.0 7.0 %collective-permute-start = (bf16[64,512]{1,0:T(8,128)(2,1)S(1)}, bf16[64,512]{1,0:T(8,128)(2,1)S(1)}, u32[]{:S(2)}, u32[]{:S(2)}) collective-permute-start(bf16[64,512]{1,0:T(8,128)(2,1)S(1)} %get-tuple-element.610), channel_id=1, source_target_pairs={{0,4},{4,8},{8,12},{12,16},{16,20},{20,24},{24,28},{28,0},{1,5},{5... | collective-permute-start | bytes 196616 | tf_op jit(solution)/shard_map/while/body/eval_jaxpr/ppermute | solution.py:9
  77.4 7.4 %all-to-all-start = ((bf16[64,4,128]{2,0,1:T(8,128)(2,1)}), bf16[64,4,128]{2,0,1:T(8,128)(2,1)S(1)}, u32[]{:S(2)}, u32[]{:S(2)}) async-start(bf16[64,4,128]{2,0,1:T(8,128)(2,1)} %copy.71), calls=%async_computation | async-start | bytes 131072 | tf_op jit(solution)/shard_map/all_to_all | solution.py:69
  80.7 89.5 %all-gather.3.cloned.1.call-start = ((), (), s32[]{:S(2)}) async-start(), calls=%async_computation.2 | async-start | bytes 8650752 | tf_op jit(solution)/shard_map/all_gather | solution.py:79
  86.8 7.6 %all-to-all-start.1 = ((bf16[4,64,128]{2,1,0:T(8,128)(2,1)}), bf16[4,64,128]{2,1,0:T(8,128)(2,1)S(1)}, u32[]{:S(2)}, u32[]{:S(2)}) async-start(bf16[4,64,128]{2,1,0:T(8,128)(2,1)} %bitcast.31), calls=%async_computation.1 | async-start | bytes 131072 | tf_op jit(solution)/shard_map/all_to_all | solution.py:81
  95.9 10.9 %collective-permute-start.1 = (f32[64,4,128]{2,1,0:T(4,128)S(1)}, f32[64,4,128]{2,1,0:T(4,128)S(1)}, u32[]{:S(2)}, u32[]{:S(2)}) collective-permute-start(f32[64,4,128]{2,1,0:T(4,128)S(1)} %get-tuple-element.652), channel_id=1, source_target_pairs={{0,4},{4,8},{8,12},{12,16},{16,20},{20,24},{24,28},{28,0},{1,5},{5... | collective-permute-start | bytes 393224 | tf_op jit(solution)/shard_map/while/body/eval_jaxpr/ppermute | solution.py:9
  107.2 7.9 %collective-permute-start.1 = (f32[64,4,128]{2,1,0:T(4,128)S(1)}, f32[64,4,128]{2,1,0:T(4,128)S(1)}, u32[]{:S(2)}, u32[]{:S(2)}) collective-permute-start(f32[64,4,128]{2,1,0:T(4,128)S(1)} %get-tuple-element.652), channel_id=1, source_target_pairs={{0,4},{4,8},{8,12},{12,16},{16,20},{20,24},{24,28},{28,0},{1,5},{5... | collective-permute-start | bytes 393224 | tf_op jit(solution)/shard_map/while/body/eval_jaxpr/ppermute | solution.py:9
  115.4 9.5 %collective-permute-start.1 = (f32[64,4,128]{2,1,0:T(4,128)S(1)}, f32[64,4,128]{2,1,0:T(4,128)S(1)}, u32[]{:S(2)}, u32[]{:S(2)}) collective-permute-start(f32[64,4,128]{2,1,0:T(4,128)S(1)} %get-tuple-element.652), channel_id=1, source_target_pairs={{0,4},{4,8},{8,12},{12,16},{16,20},{20,24},{24,28},{28,0},{1,5},{5... | collective-permute-start | bytes 393224 | tf_op jit(solution)/shard_map/while/body/eval_jaxpr/ppermute | solution.py:9
  125.3 9.7 %collective-permute-start.1 = (f32[64,4,128]{2,1,0:T(4,128)S(1)}, f32[64,4,128]{2,1,0:T(4,128)S(1)}, u32[]{:S(2)}, u32[]{:S(2)}) collective-permute-start(f32[64,4,128]{2,1,0:T(4,128)S(1)} %get-tuple-element.652), channel_id=1, source_target_pairs={{0,4},{4,8},{8,12},{12,16},{16,20},{20,24},{24,28},{28,0},{1,5},{5... | collective-permute-start | bytes 393224 | tf_op jit(solution)/shard_map/while/body/eval_jaxpr/ppermute | solution.py:9
  135.4 10.5 %collective-permute-start.1 = (f32[64,4,128]{2,1,0:T(4,128)S(1)}, f32[64,4,128]{2,1,0:T(4,128)S(1)}, u32[]{:S(2)}, u32[]{:S(2)}) collective-permute-start(f32[64,4,128]{2,1,0:T(4,128)S(1)} %get-tuple-element.652), channel_id=1, source_target_pairs={{0,4},{4,8},{8,12},{12,16},{16,20},{20,24},{24,28},{28,0},{1,5},{5... | collective-permute-start | bytes 393224 | tf_op jit(solution)/shard_map/while/body/eval_jaxpr/ppermute | solution.py:9
  146.2 10.9 %collective-permute-start.1 = (f32[64,4,128]{2,1,0:T(4,128)S(1)}, f32[64,4,128]{2,1,0:T(4,128)S(1)}, u32[]{:S(2)}, u32[]{:S(2)}) collective-permute-start(f32[64,4,128]{2,1,0:T(4,128)S(1)} %get-tuple-element.652), channel_id=1, source_target_pairs={{0,4},{4,8},{8,12},{12,16},{16,20},{20,24},{24,28},{28,0},{1,5},{5... | collective-permute-start | bytes 393224 | tf_op jit(solution)/shard_map/while/body/eval_jaxpr/ppermute | solution.py:9
  157.5 10.3 %collective-permute-start.1 = (f32[64,4,128]{2,1,0:T(4,128)S(1)}, f32[64,4,128]{2,1,0:T(4,128)S(1)}, u32[]{:S(2)}, u32[]{:S(2)}) collective-permute-start(f32[64,4,128]{2,1,0:T(4,128)S(1)} %get-tuple-element.652), channel_id=1, source_target_pairs={{0,4},{4,8},{8,12},{12,16},{16,20},{20,24},{24,28},{28,0},{1,5},{5... | collective-permute-start | bytes 393224 | tf_op jit(solution)/shard_map/while/body/eval_jaxpr/ppermute | solution.py:9
Sparse Core Ops, SparseCore 0:
  86.0 84.1 all-gather.2
